TPU v7x, 256 devices: a whole 4x4x8 slice. The times are simulated.
256 devices in a mesh: tm: 64 (over x, z, core), tmpl: 4 (over y).
Axes of the slice: x: 4, y: 4, z: 8, core: 2. Of those that a mesh axis runs over, the one named last changes fastest.
Arguments:
- records: float32 [4, 36864, 512], P('tmpl', 'tm'), may hold values from -6 to 6
- band_filter: float32 [65], replicated, may hold values from -0.75 to 0.75
- templates: bfloat16 [1024, 144, 128], P('tmpl'), may hold values from -6 to 6
- destinations: int32 [4, 36864], P('tmpl', 'tm'), may hold values from 0 to 63, as said below
- offsets: int32 [4, 36864], P('tmpl', 'tm'), may hold values from 0 to 294400, as said below
- live_counts: int32 [4, 64], P('tmpl', 'tm'), may hold values from 9 to 576, as said below
Outputs:
- detection: float32 [1024, 65536], P('tmpl', 'tm')
Inputs may be any that keep to these rules, and one draw needn't show every extreme that they name: `destinations`: device s's 576 entries of a quarter name every window exactly 9 times, so at most 9 live records go from one device to one window; in each quarter some window has all its entries live on every device. `offsets`: multiples of 512; within a quarter every pair of destination and offset occurs exactly once over all entries of all devices. The live entries of a device are its first live_counts entries; the others are absent records.
All inputs are finite; a program needn't handle non-finite values.
Results may differ from a plain program's by a relative error of at most 0.0029.
Values may be sent and summed in bfloat16 or wider, within the bound.
A program may use at most 128 MiB of HBM per device.

v0:
```python
import math

import jax
import jax.numpy as jnp
from jax import lax
from jax.sharding import PartitionSpec as P

CH = 144
DEC = 8
TAPS = 65


EPSILON = 1e-06


def side_by_side(arrays, axis, split_dim, concat_dim, along):
    widths = [math.prod(a.shape[along:]) for a in arrays]
    both = jnp.concatenate(
        [a.reshape(*a.shape[:along], w) for a, w in zip(arrays, widths)], axis=along
    )
    result = lax.all_to_all(both, axis, split_axis=split_dim, concat_axis=concat_dim, tiled=True)
    blocks = jnp.split(result, [sum(widths[:k]) for k in range(1, len(widths))], axis=along)
    return tuple(
        (b.reshape(*result.shape[:along], *a.shape[along:]) for a, b in zip(arrays, blocks))
    )


def passed_along(value, axis, steps):
    count = lax.axis_size(axis)
    initial, last = (max(0, -steps), min(count, count - steps))
    return lax.ppermute(value, axis, [(source, source + steps) for source in range(initial, last)])


def joined_along(blocks, dim):
    shape = list(blocks.shape[1:])
    shape[dim] *= blocks.shape[0]
    return jnp.moveaxis(blocks, 0, dim).reshape(shape)


def sent_to_all(shard, axis):
    copies = jnp.broadcast_to(shard, (lax.axis_size(axis), *shard.shape))
    return lax.all_to_all(copies, axis, split_axis=0, concat_axis=0, tiled=True)


def gather_directly(shard, axis, dim):
    return joined_along(sent_to_all(shard, axis), dim)


def filter_phases(source, band_filter, count):
    rows = source.shape[0]
    blocks = (band_filter.shape[0] + DEC - 1) // DEC
    frames = count + blocks - 1
    needed = DEC * frames
    source = jnp.pad(source, ((0, 0), (0, needed - source.shape[1])))
    phased = source.reshape(rows, frames, DEC).transpose(0, 2, 1)
    taps_padded = jnp.pad(band_filter, (0, blocks * DEC - band_filter.shape[0])).reshape(
        blocks, DEC
    )
    result = jnp.zeros((rows, count), jnp.float32)
    for block in range(blocks):
        result = result + jnp.einsum(
            "rbn,b->rn",
            phased[:, :, block : block + count],
            taps_padded[block],
            precision=lax.Precision.HIGHEST,
        )
    return result


def arrange(arrived, arrived_labels, entries):
    flat = arrived.reshape(-1, arrived.shape[-1])
    names = arrived_labels.reshape(-1)
    target = jnp.where(names >= 0, names, entries).astype(jnp.int32)
    empty = jnp.zeros((entries + 1, flat.shape[1]), jnp.float32)
    return empty.at[target].set(flat)[:-1]


def shards(records, band_filter, templates, destinations, offsets, live_counts):
    stored = records[0]
    targets = destinations[0]
    starts = offsets[0]
    number = live_counts[0, 0]
    devices = lax.axis_size("tm")
    entries, rec_len = stored.shape
    capacity = entries // devices
    channels_here = CH // lax.axis_size("tmpl")
    slot_count = entries // channels_here
    window_len = slot_count * rec_len // DEC
    heads_len = (TAPS - 1) // DEC
    is_live = jnp.arange(entries, dtype=jnp.int32) < number
    member = (
        (targets[:, None] == jnp.arange(devices, dtype=jnp.int32)[None, :]) & is_live[:, None]
    ).astype(jnp.int32)
    order_in = jnp.sum(jnp.cumsum(member, 0) * member, 1) - 1
    placed = jnp.where(is_live, targets * capacity + order_in, devices * capacity)
    labels = (starts // rec_len).astype(jnp.float32)
    label_buf = (
        jnp.full((devices * capacity + 1,), -1.0, jnp.float32)
        .at[placed]
        .set(labels)[:-1]
        .reshape(devices, capacity)
    )
    padded = jnp.pad(stored, ((0, 0), (TAPS - 1, 0)))
    span = rec_len // DEC + heads_len
    partial_value = filter_phases(padded, band_filter, span)
    outgoing = (
        jnp.zeros((devices * capacity + 1, span), jnp.float32)
        .at[placed]
        .set(partial_value)[:-1]
        .reshape(devices, capacity, span)
    )
    arrived, arrived_labels = side_by_side((outgoing, label_buf), "tm", 0, 0, 2)
    local = arrange(arrived, arrived_labels, entries).reshape(channels_here, slot_count, span)
    head_part = local[:, :, :heads_len]
    tail_part = local[:, :, heads_len:]
    following = passed_along(head_part[:, 0, :], "tm", -1)
    later = jnp.concatenate([head_part[:, 1:, :], following[:, None, :]], 1)
    tail_part = tail_part.at[:, :, rec_len // DEC - heads_len :].add(later)
    filtered = tail_part.reshape(channels_here, window_len)
    decim = filtered.astype(jnp.bfloat16)
    tlen = templates.shape[2]
    kept = templates.shape[0]
    width = min(16, tlen)
    after = passed_along(decim[:, : tlen - 1], "tm", -1)
    window_data = jnp.concatenate([decim, after], 1)
    piece = gather_directly(window_data, "tmpl", 0)
    corr = jnp.zeros((kept, window_len), jnp.float32)
    rows = piece.shape[0]

    def add_group(group, total):
        first = group * width
        block_tmpl = lax.dynamic_slice_in_dim(templates, first, width, 2).reshape(
            kept, rows * width
        )
        shifted = jnp.stack(
            [
                lax.dynamic_slice_in_dim(piece, first + shift_at, window_len, 1)
                for shift_at in range(width)
            ],
            1,
        )
        shifted = shifted.reshape(rows * width, window_len)
        return total + jnp.dot(block_tmpl, shifted, preferred_element_type=jnp.float32)

    corr = lax.fori_loop(0, tlen // width, add_group, corr)
    wide_piece = piece.astype(jnp.float32)
    corr, power = (corr, jnp.sum(wide_piece * wide_piece, 0))
    running = jnp.concatenate([jnp.zeros((1,), jnp.float32), jnp.cumsum(power)])
    energy = (running[tlen:] - running[:window_len]) / (CH * tlen)
    tscale = jnp.sqrt(jnp.mean(jnp.square(templates.astype(jnp.float32)), axis=(1, 2)) + EPSILON)
    return corr / (CH * tlen * tscale[:, None] * jnp.sqrt(energy + EPSILON)[None, :])


def solution(mesh):
    in_specs = (
        P("tmpl", "tm", None),
        P(),
        P("tmpl", None, None),
        P("tmpl", "tm"),
        P("tmpl", "tm"),
        P("tmpl", "tm"),
    )
    out_specs = P("tmpl", "tm")
    return jax.shard_map(shards, mesh=mesh, in_specs=in_specs, out_specs=out_specs, check_vma=False)
```

profile of v0, /device:TPU:1, one launch (start us, length us, event | category | flops | bytes accessed | tf_op | source)
XLA Modules:
  0.0 248.8 jit_solution(13263341122409007318)
XLA Ops:
  0.0 1.7 copy.35
  1.7 2.0 fusion.11
  3.7 2.0 fusion.10
  19.8 4.6 %scatter_custom_fusion = f32[577,72]{1,0:T(8,128)S(1)} fusion(s32[576]{0:T(1024)S(1)} %fusion.27, f32[1,576,72]{2,1,0:T(8,128)S(1)} %copy.48, f32[1,576,72]{2,1,0:T(8,128)S(1)} %copy.47, f32[1,576,72]{2,1,0:T(8,128)S(1)} %copy.46, f32[1,576,72]{2,1,0:T(8,128)S(1)} %copy.45, f32[1,576,72]{2,1,0:T(8,128)S(1)} %copy.44, f32[1,576,72]{2,1,0:T(8,128)S(1)} %copy.43, ...), kind=kCustom, calls=%fused_computation.40 | custom fusion | flops 331776 | bytes 2820388 | tf_op jit(solution)/shard_map/scatter | solution.py:109
  24.5 4.1 %scatter_custom_fusion.1 = f32[577]{0:T(1024)S(1)} fusion(s32[576]{0:T(1024)S(1)} %fusion.27, f32[576]{0:T(1024)S(1)} %fusion.21, f32[]{:T(128)} %constant.299.clone.1), kind=kCustom, calls=%fused_computation.89 | custom fusion | bytes 2312 | tf_op jit(solution)/shard_map/scatter | solution.py:100
  29.4 23.7 %all_to_all.10 = f32[64,1,657]{2,1,0:T(1,128)S(1)} all-to-all(f32[64,1,657]{2,1,0:T(1,128)S(1)} %reshape.249), channel_id=1, replica_groups=mesh['tm'=64,'tmpl'=4] {'tm'}, dimensions={0} | all-to-all | bytes 336384 | tf_op jit(solution)/shard_map/all_to_all | solution.py:21
  55.6 4.2 %scatter_custom_fusion.2 = f32[577,72]{1,0:T(8,128)S(1)} fusion(s32[576]{0:T(1024)S(1)} %fusion.28, f32[576,72]{1,0:T(8,128)S(1)} %reshape.213, f32[]{:T(128)} %constant.293.clone.1), kind=kCustom, calls=%fused_computation.60 | custom fusion | bytes 166180 | tf_op jit(solution)/shard_map/scatter | solution.py:75
  59.9 2.4 collective-permute-start
  62.5 2.4 collective-permute-done
  65.1 6.9 %scatter-add.4 = bf16[36,16,64]{2,1,0:T(8,128)(2,1)S(1)} dynamic-update-slice(bf16[36,16,64]{2,1,0:T(8,128)(2,1)S(1)} %slice.184, bf16[36,16,8]{2,1,0:T(8,128)(2,1)S(1)} %slice_add_fusion, s32[]{:T(128)} %constant.292.clone.1, s32[]{:T(128)} %constant.292.clone.1, s32[]{:T(128)} %constant.303.clone.1) | dynamic-update-slice | bytes 18436 | tf_op jit(solution)/shard_map/scatter-add | solution.py:118
  72.1 1.9 collective-permute-start.1
  74.1 3.1 %collective-permute-done.1 = bf16[36,127]{1,0:T(8,128)(2,1)S(1)} collective-permute-done((bf16[36,127]{1,0:T(8,128)(2,1)S(1)}, bf16[36,127]{1,0:T(8,128)(2,1)S(1)}, u32[]{:S(2)}, u32[]{:S(2)}) %collective-permute-start.1) | collective-permute-done | bytes 9176 | tf_op jit(solution)/shard_map/ppermute | solution.py:31
  77.9 4.2 %all-to-all-start.1 = ((bf16[4,36,1151]{2,1,0:T(8,128)(2,1)}), bf16[4,36,1151]{2,1,0:T(8,128)(2,1)S(1)}, u32[]{:S(2)}, u32[]{:S(2)}) async-start(bf16[4,36,1151]{2,1,0:T(8,128)(2,1)} %broadcast_in_dim.32), calls=%async_computation.1 | async-start | bytes 737280 | tf_op jit(solution)/shard_map/all_to_all | solution.py:42
  82.1 5.9 %multiply_reduce_fusion = f32[256]{0:T(256)S(1)} fusion(bf16[256,144,128]{2,1,0:T(8,128)(2,1)} %param.12), kind=kLoop, calls=%fused_computation.23 | loop fusion | flops 14155520 | bytes 9438208 | tf_op jit(solution)/shard_map/reduce_sum | solution.py:150
  88.0 13.9 %copy.39 = bf16[256,144,128]{0,1,2:T(8,128)(2,1)} copy(bf16[256,144,128]{2,1,0:T(8,128)(2,1)} %param.12) | data formatting | bytes 18874368
  102.7 144.8 %while.17 = (s32[]{:T(128)}, f32[256,1024]{1,0:T(8,128)S(1)}, bf16[256,144,128]{0,1,2:T(8,128)(2,1)}, bf16[144,1151]{1,0:T(8,128)(2,1)S(1)}, s32[]{:T(128)}, /*i...) while((s32[]{:T(128)}, f32[256,1024]{1,0:T(8,128)S(1)}, ...), condition=%wide.region_7.8_spmd.clone, body=%wide.region_6.7_spmd.clone.sunk | while | flops 1208483968 | bytes 17433740 | solution.py:145
  116.6 4.2 %fusion.66 = f32[256,1024]{1,0:T(8,128)S(1)} fusion(bf16[144,16,1024]{2,0,1:T(8,128)(2,1)} %bitcast_dynamic-update-slice_fusion.47, bf16[256,144,128]{0,1,2:T(8,128)(2,1)} %get-tuple-element.288, s32[]{:T(128)S(6)} %select_n.290, f32[256,1024]{1,0:T(8,128)S(1)} %get-tuple-element.249, pred[]{:T(512)S(6)} %compare.15), kind=kOutput, calls=%fused_computation.4.clone.1 | convolution fusion | flops 1208483840 | bytes 7995397 | tf_op jit(solution)/shard_map/while/body/eval_jaxpr/dot_general | solution.py:143
  134.7 4.2 %fusion.66 = f32[256,1024]{1,0:T(8,128)S(1)} fusion(bf16[144,16,1024]{2,0,1:T(8,128)(2,1)} %bitcast_dynamic-update-slice_fusion.47, bf16[256,144,128]{0,1,2:T(8,128)(2,1)} %get-tuple-element.288, s32[]{:T(128)S(6)} %select_n.290, f32[256,1024]{1,0:T(8,128)S(1)} %get-tuple-element.249, pred[]{:T(512)S(6)} %compare.15), kind=kOutput, calls=%fused_computation.4.clone.1 | convolution fusion | flops 1208483840 | bytes 7995397 | tf_op jit(solution)/shard_map/while/body/eval_jaxpr/dot_general | solution.py:143
  152.8 4.2 %fusion.66 = f32[256,1024]{1,0:T(8,128)S(1)} fusion(bf16[144,16,1024]{2,0,1:T(8,128)(2,1)} %bitcast_dynamic-update-slice_fusion.47, bf16[256,144,128]{0,1,2:T(8,128)(2,1)} %get-tuple-element.288, s32[]{:T(128)S(6)} %select_n.290, f32[256,1024]{1,0:T(8,128)S(1)} %get-tuple-element.249, pred[]{:T(512)S(6)} %compare.15), kind=kOutput, calls=%fused_computation.4.clone.1 | convolution fusion | flops 1208483840 | bytes 7995397 | tf_op jit(solution)/shard_map/while/body/eval_jaxpr/dot_general | solution.py:143
  170.9 4.2 %fusion.66 = f32[256,1024]{1,0:T(8,128)S(1)} fusion(bf16[144,16,1024]{2,0,1:T(8,128)(2,1)} %bitcast_dynamic-update-slice_fusion.47, bf16[256,144,128]{0,1,2:T(8,128)(2,1)} %get-tuple-element.288, s32[]{:T(128)S(6)} %select_n.290, f32[256,1024]{1,0:T(8,128)S(1)} %get-tuple-element.249, pred[]{:T(512)S(6)} %compare.15), kind=kOutput, calls=%fused_computation.4.clone.1 | convolution fusion | flops 1208483840 | bytes 7995397 | tf_op jit(solution)/shard_map/while/body/eval_jaxpr/dot_general | solution.py:143
  189.0 4.2 %fusion.66 = f32[256,1024]{1,0:T(8,128)S(1)} fusion(bf16[144,16,1024]{2,0,1:T(8,128)(2,1)} %bitcast_dynamic-update-slice_fusion.47, bf16[256,144,128]{0,1,2:T(8,128)(2,1)} %get-tuple-element.288, s32[]{:T(128)S(6)} %select_n.290, f32[256,1024]{1,0:T(8,128)S(1)} %get-tuple-element.249, pred[]{:T(512)S(6)} %compare.15), kind=kOutput, calls=%fused_computation.4.clone.1 | convolution fusion | flops 1208483840 | bytes 7995397 | tf_op jit(solution)/shard_map/while/body/eval_jaxpr/dot_general | solution.py:143
  207.1 4.2 %fusion.66 = f32[256,1024]{1,0:T(8,128)S(1)} fusion(bf16[144,16,1024]{2,0,1:T(8,128)(2,1)} %bitcast_dynamic-update-slice_fusion.47, bf16[256,144,128]{0,1,2:T(8,128)(2,1)} %get-tuple-element.288, s32[]{:T(128)S(6)} %select_n.290, f32[256,1024]{1,0:T(8,128)S(1)} %get-tuple-element.249, pred[]{:T(512)S(6)} %compare.15), kind=kOutput, calls=%fused_computation.4.clone.1 | convolution fusion | flops 1208483840 | bytes 7995397 | tf_op jit(solution)/shard_map/while/body/eval_jaxpr/dot_general | solution.py:143
  225.2 4.2 %fusion.66 = f32[256,1024]{1,0:T(8,128)S(1)} fusion(bf16[144,16,1024]{2,0,1:T(8,128)(2,1)} %bitcast_dynamic-update-slice_fusion.47, bf16[256,144,128]{0,1,2:T(8,128)(2,1)} %get-tuple-element.288, s32[]{:T(128)S(6)} %select_n.290, f32[256,1024]{1,0:T(8,128)S(1)} %get-tuple-element.249, pred[]{:T(512)S(6)} %compare.15), kind=kOutput, calls=%fused_computation.4.clone.1 | convolution fusion | flops 1208483840 | bytes 7995397 | tf_op jit(solution)/shard_map/while/body/eval_jaxpr/dot_general | solution.py:143
  243.3 4.2 %fusion.66 = f32[256,1024]{1,0:T(8,128)S(1)} fusion(bf16[144,16,1024]{2,0,1:T(8,128)(2,1)} %bitcast_dynamic-update-slice_fusion.47, bf16[256,144,128]{0,1,2:T(8,128)(2,1)} %get-tuple-element.288, s32[]{:T(128)S(6)} %select_n.290, f32[256,1024]{1,0:T(8,128)S(1)} %get-tuple-element.249, pred[]{:T(512)S(6)} %compare.15), kind=kOutput, calls=%fused_computation.4.clone.1 | convolution fusion | flops 1208483840 | bytes 7995397 | tf_op jit(solution)/shard_map/while/body/eval_jaxpr/dot_general | solution.py:143
  (199 shorter events, 131.1 us)
Async XLA Ops:
  0.0 5.7 %copy-start = (f32[65]{0:T(128)S(1)}, f32[65]{0:T(128)}, u32[]{:S(2)}) copy-start(f32[65]{0:T(128)} %param.11) | copy-start | bytes 784
  7.1 9.1 %copy-start.1 = (s32[1,576]{1,0:T(1,128)S(1)}, s32[1,576]{1,0:T(1,128)}, u32[]{:S(2)}) copy-start(s32[1,576]{1,0:T(1,128)} %param.13) | copy-start | bytes 6916
  17.8 6.7 %copy-start.2 = (s32[1,576]{1,0:T(1,128)S(1)}, s32[1,576]{1,0:T(1,128)}, u32[]{:S(2)}) copy-start(s32[1,576]{1,0:T(1,128)} %param.14) | copy-start | bytes 6916
  59.9 4.9 %collective-permute-start = (f32[36,8]{0,1:T(8,128)S(1)}, f32[36,8]{0,1:T(8,128)S(1)}, u32[]{:S(2)}, u32[]{:S(2)}) collective-permute-start(f32[36,8]{0,1:T(8,128)S(1)} %bitcast.204), channel_id=1, source_target_pairs={{4,0},{8,4},{12,8},{16,12},{20,16},{24,20},{28,24},{32,28},{36,32}... | collective-permute-start | bytes 3464 | tf_op jit(solution)/shard_map/ppermute | solution.py:31
  72.1 5.0 %collective-permute-start.1 = (bf16[36,127]{1,0:T(8,128)(2,1)S(1)}, bf16[36,127]{1,0:T(8,128)(2,1)S(1)}, u32[]{:S(2)}, u32[]{:S(2)}) collective-permute-start(bf16[36,127]{1,0:T(8,128)(2,1)S(1)} %slice.188), channel_id=1, source_target_pairs={{4,0},{8,4},{12,8},{16,12},{20,16},{24,20},{28,24},{32,28},{36,32}... | collective-permute-start | bytes 27440 | tf_op jit(solution)/shard_map/ppermute | solution.py:31
  77.9 24.0 %all-to-all-start.1 = ((bf16[4,36,1151]{2,1,0:T(8,128)(2,1)}), bf16[4,36,1151]{2,1,0:T(8,128)(2,1)S(1)}, u32[]{:S(2)}, u32[]{:S(2)}) async-start(bf16[4,36,1151]{2,1,0:T(8,128)(2,1)} %broadcast_in_dim.32), calls=%async_computation.1 | async-start | bytes 737280 | tf_op jit(solution)/shard_map/all_to_all | solution.py:42
where the time goes:
time: 250 us; the launch traced here: 249 us
  local copies, waits for them, and re-layouts  147 us (59%)
  matrix products  47.2 us (19%)
  blocking collectives  23.7 us (9%)
  other arithmetic  15.5 us (6%)
  starting transfers between devices  8.53 us (3%)
  waiting for transfers between devices  5.42 us (2%)
    while x120, local copies, waits for them, and re-layouts  104 us
    dot_general x8, matrix products, add_group(): jnp.dot(block_tmpl, shifted, preferred_element_type=jnp.float32)  33.4 us
    all_to_all x1, blocking collectives, side_by_side(): lax.all_to_all(both, axis, split_axis=split_dim, concat_axis=concat_dim,...  23.7 us
    unnamed x10, local copies, waits for them, and re-layouts  16.3 us
    dot_general x9, matrix products, filter_phases(): jnp.einsum('rbn,b->rn', phased[:, :, block:block + count], taps_padded[bl...  13.7 us
    scatter-add x1, local copies, waits for them, and re-layouts, shards(): tail_part = tail_part.at[:, :, rec_len // DEC - heads_len:].add(later)  6.88 us
    another operation x8, local copies, waits for them, and re-layouts, add_group(): jnp.stack([lax.dynamic_slice_in_dim(piece, first + shift_at, window_len,...  6.82 us
    reduce_sum x1, other arithmetic, shards(): jnp.mean(jnp.square(templates.astype(jnp.float32)), axis=(1, 2)) + EPSILON  5.85 us
  transfers between devices with their start and end apart: 3, of which 2 were waited for; matrix products, arithmetic and copies ran while one was open for 8% of the time, Pallas kernels for 0%

commit v1 on v0

v1 whole, which is shorter than its diff:
```python
import jax
import jax.numpy as jnp
from jax import lax
from jax.experimental import pallas as pl
from jax.experimental.pallas import tpu as pltpu
from jax.sharding import PartitionSpec as P

CH = 144
TAPS = 65
DEC = 8
RECLEN = 512
TLEN = 128
EPSILON = 1e-06

NTM = 64
NY = 4
ENT = 576
EPAD = 640
CAP = 16
UNITS = 3
UCH = 12
KEPT = 256
WIN = 1024
F32 = jnp.float32
BF16 = jnp.bfloat16
MESH = pl.DeviceIdType.MESH
NT = (((1,), (1,)), ((), ()))


def iota(shape, dim):
    return lax.broadcasted_iota(jnp.int32, shape, dim)


def lane_take(x, index):
    return jnp.take_along_axis(x, index, axis=1)


def kernel(
    dest_ref,
    offs_ref,
    live_ref,
    band_ref,
    rec_hbm,
    tmpl_hbm,
    out_ref,
    rec,
    tmpl,
    taps,
    rows,
    ybuf,
    send,
    arr,
    wts,
    tsq,
    gall,
    g32,
    pw,
    hank,
    acc,
    rec_sem,
    tmpl_sem,
    a_send,
    a_recv,
    b_send,
    main_recv,
    halo_recv,
):
    me = lax.axis_index("tm")
    my = lax.axis_index("tmpl")

    rec_copy = pltpu.make_async_copy(rec_hbm.at[0], rec.at[pl.ds(0, ENT)], rec_sem)
    rec_copy.start()
    barrier = pltpu.get_barrier_semaphore()

    def greet(i, _):
        pl.semaphore_signal(
            barrier, inc=1, device_id={"tm": lax.rem(me + i, NTM)}, device_id_type=MESH
        )
        return 0

    lax.fori_loop(1, NTM, greet, 0)
    for i in range(1, NY):
        other = lax.rem(my + i, NY)
        pl.semaphore_signal(barrier, inc=1, device_id={"tmpl": other}, device_id_type=MESH)

        @pl.when(me < NTM - 1)
        def _():
            pl.semaphore_signal(
                barrier, inc=1, device_id={"tm": me + 1, "tmpl": other}, device_id_type=MESH
            )

    def tmpl_copy(b):
        part = pl.ds(pl.multiple_of(b * 16, 16), 16)
        return pltpu.make_async_copy(tmpl_hbm.at[part], tmpl.at[part], tmpl_sem.at[b])

    for b in range(16):
        tmpl_copy(b).start()

    rec[ENT:EPAD, :] = jnp.zeros((EPAD - ENT, RECLEN), F32)
    rows[...] = jnp.full(rows.shape, -1, jnp.int32)
    rows[0:1, 0:ENT] = dest_ref[...]
    rows[1:2, 0:ENT] = offs_ref[...]
    entry = iota((1, EPAD), 1)
    target = rows[0:1, :]
    label = jnp.maximum(rows[1:2, :], 0) // RECLEN
    chan = label // 16
    slot = label - chan * 16
    chan = chan + 4 * (chan // UCH)
    member = jnp.where(jnp.broadcast_to(target, (NTM, EPAD)) == iota((NTM, EPAD), 0), 1.0, 0.0)
    before = jnp.where(iota((EPAD, EPAD), 0) < iota((EPAD, EPAD), 1), 1.0, 0.0).astype(BF16)
    ahead = jnp.dot(member.astype(BF16), before, preferred_element_type=F32)
    rank = jnp.sum(ahead * member, axis=0, keepdims=True).astype(jnp.int32)
    live = entry < jnp.minimum(live_ref[0, 0], ENT)
    place = jnp.where(live, target * CAP + rank, -1)

    taps[...] = jnp.zeros(taps.shape, F32)
    taps[0:1, 0:TAPS] = band_ref[...]
    line = jnp.broadcast_to(taps[0:1, :], (80, 128))
    parts = []
    for s in range(4):
        tap = iota((80, 128), 1) + 128 * s + DEC * iota((80, 128), 0) - (RECLEN - DEC)
        good = (tap >= 0) & (tap < TAPS) & (iota((80, 128), 0) < 72)
        parts.append(jnp.where(good, lane_take(line, jnp.clip(tap, 0, 127)), 0.0))
    band = jnp.concatenate(parts, axis=1)
    band_hi = band.astype(BF16)
    band_lo = (band - band_hi.astype(F32)).astype(BF16)

    rec_copy.wait()
    data = rec[...]
    data_hi = data.astype(BF16)
    data_lo = (data - data_hi.astype(F32)).astype(BF16)
    parts = lax.dot_general(band_hi, data_hi, NT, preferred_element_type=F32)
    parts += lax.dot_general(band_hi, data_lo, NT, preferred_element_type=F32)
    parts += lax.dot_general(band_lo, data_hi, NT, preferred_element_type=F32)
    row = iota((80, EPAD), 0)
    parts = jnp.where(row == 72, jnp.broadcast_to(chan.astype(F32), (80, EPAD)), parts)
    parts = jnp.where(row == 73, jnp.broadcast_to(slot.astype(F32), (80, EPAD)), parts)
    parts = jnp.concatenate([parts, jnp.zeros((48, EPAD), F32)], axis=0).astype(BF16)

    ybuf[NTM * CAP :, :] = jnp.zeros((CAP, 128), F32)
    for q in range(4):
        pick = jnp.where(
            jnp.broadcast_to(place, (256, EPAD)) == iota((256, EPAD), 0) + 256 * q, 1.0, 0.0
        ).astype(BF16)
        ybuf[256 * q : 256 * q + 256, :] = lax.dot_general(
            pick, parts, NT, preferred_element_type=F32
        )
    lane = iota((256, 128), 1)
    for q in range(4):
        own = ybuf[256 * q : 256 * q + 256, :]
        after = ybuf[256 * q + CAP : 256 * q + 256 + CAP, :]
        both = jnp.where((lane >= 80) & (lane < 90), pltpu.roll(after, 16, 1), own)
        send[16 * q : 16 * q + 16] = both.astype(BF16).reshape(16, CAP, 128)

    pl.semaphore_wait(barrier, 66 + jnp.where(me > 0, 3, 0))

    def block_copy(to, frm):
        return pltpu.make_async_remote_copy(
            src_ref=send.at[to],
            dst_ref=arr.at[frm],
            send_sem=a_send,
            recv_sem=a_recv,
            device_id={"tm": to},
            device_id_type=MESH,
        )

    def send_block(i, _):
        block_copy(lax.rem(me + i, NTM), me).start()
        return 0

    lax.fori_loop(1, NTM, send_block, 0)
    arr[me] = send[me]

    def order_templates(b, _):
        tmpl_copy(b).wait()
        part = pl.ds(pl.multiple_of(b * 16, 16), 16)
        total = jnp.zeros((16, 16, 128), F32)
        for g in range(9):
            x = tmpl[part, 16 * g : 16 * g + 16, :]
            wts[16 * g : 16 * g + 16, part, :] = jnp.transpose(x, (1, 0, 2))
            wide = x.astype(F32)
            total = total + wide * wide
        tsq[part, :] = jnp.sum(total, axis=1)
        return 0

    lax.fori_loop(0, 16, order_templates, 0)

    def all_blocks():
        return pltpu.make_async_remote_copy(
            src_ref=send.at[pl.ds(0, NTM - 1)],
            dst_ref=arr.at[pl.ds(0, NTM - 1)],
            send_sem=a_send,
            recv_sem=a_recv,
            device_id={"tm": me},
            device_id_type=MESH,
        )

    all_blocks().wait_recv()

    came = arr[...].reshape(NTM * CAP, 128)
    sel_row = iota((8, 128), 0)
    sel_lane = iota((8, 128), 1)
    selector = (
        ((sel_row == 0) & (sel_lane == 72))
        | ((sel_row == 1) & (sel_lane == 73))
        | ((sel_row == 2) & (sel_lane == 88))
        | ((sel_row == 3) & (sel_lane == 89))
    )
    names = lax.dot_general(
        jnp.where(selector, 1.0, 0.0).astype(BF16), came, NT, preferred_element_type=F32
    ).astype(jnp.int32)
    spot = names[0:1, :] + 48 * (15 - names[1:2, :])
    spot_next = jnp.where(names[3:4, :] == 0, names[2:3, :], -1)
    lane = iota((48, 128), 1)
    pick = jnp.where(
        jnp.broadcast_to(spot_next, (48, 1024)) == iota((48, 1024), 0), 1.0, 0.0
    ).astype(BF16)
    carry = pltpu.roll(jnp.dot(pick, came, preferred_element_type=F32), 48, 1)
    for b in range(8):
        pick = jnp.where(
            jnp.broadcast_to(spot, (96, 1024)) == iota((96, 1024), 0) + 96 * b, 1.0, 0.0
        ).astype(BF16)
        got = jnp.dot(pick, came, preferred_element_type=F32)
        odd = pltpu.roll(got[48:96], 64, 1)
        block = (
            jnp.where(lane < 72, got[0:48], 0.0)
            + jnp.where(lane >= 64, odd, 0.0)
            + jnp.where(lane < 8, carry, 0.0)
        )
        carry = odd
        gall[my, :, :, 128 * (b + 1) : 128 * (b + 2)] = block.astype(BF16).reshape(UNITS, 16, 128)

    @pl.when(me == NTM - 1)
    def _():
        gall[:, :, :, 0:128] = jnp.zeros((NY, UNITS, 16, 128), BF16)

    def halo_copy(quarter, to_tm, to_y, k=0):
        return pltpu.make_async_remote_copy(
            src_ref=gall.at[quarter, :, :, pl.ds(WIN, 128)],
            dst_ref=gall.at[quarter, :, :, pl.ds(0, 128)],
            send_sem=b_send.at[4 + k],
            recv_sem=halo_recv.at[quarter],
            device_id={"tm": to_tm, "tmpl": to_y},
            device_id_type=MESH,
        )

    def main_copy(quarter, to_y, k=0):
        return pltpu.make_async_remote_copy(
            src_ref=gall.at[quarter, :, :, pl.ds(128, WIN)],
            dst_ref=gall.at[quarter, :, :, pl.ds(128, WIN)],
            send_sem=b_send.at[k],
            recv_sem=main_recv.at[quarter],
            device_id={"tmpl": to_y},
            device_id_type=MESH,
        )

    @pl.when(me > 0)
    def _():
        for i in (0, 1, 3, 2):
            halo_copy(my, me - 1, lax.rem(my + i, NY), i).start()

    for i in (1, 3, 2):
        main_copy(my, lax.rem(my + i, NY), i).start()

    def quarter_of(n):
        step = n // UNITS
        return lax.rem(my + lax.bitwise_xor(step, lax.shift_right_logical(step, 1)), NY)

    def arrive(n, mine):
        quarter = quarter_of(n)
        if not mine:
            main_copy(quarter, my).wait_recv()

        @pl.when(me < NTM - 1)
        def _():
            halo_copy(quarter, me, my).wait_recv()

    hl = iota((16, 128), 1)
    hr = iota((16, 128), 0)

    def build(n, side):
        wide = gall[quarter_of(n), lax.rem(n, UNITS)].astype(F32)
        g32[side] = wide
        pw[...] += wide * wide
        for i in range(UCH):
            line = [
                jnp.broadcast_to(g32[side, i : i + 1, 128 * b : 128 * b + 128], (16, 128))
                for b in range(9)
            ]
            for s in range(8):
                from_next = hl >= hr + 16 * s
                turned = [pltpu.roll(x, 16 * s, 1, stride=1, stride_axis=0) for x in line]
                for b in range(8):
                    at = i * 128 + 16 * s
                    hank[side, at : at + 16, 128 * b : 128 * b + 128] = jnp.where(
                        from_next, turned[b + 1], turned[b]
                    ).astype(BF16)

    def correlate(n, side):
        c0 = quarter_of(n) * (CH // NY) + lax.rem(n, UNITS) * UCH
        left = jnp.concatenate([wts[c0 + i] for i in range(UCH)], axis=1)
        acc[...] += jnp.dot(left, hank[side], preferred_element_type=F32)

    acc[...] = jnp.zeros(acc.shape, F32)
    pw[...] = jnp.zeros(pw.shape, F32)
    arrive(0, True)
    build(0, 0)
    total_units = NY * UNITS

    def step(it, _):
        n = 2 * it

        @pl.when((it == 1) | (it == 4))
        def _():
            arrive(n + 1, False)

        build(n + 1, 1)
        correlate(n, 0)

        @pl.when(it == 2)
        def _():
            arrive(n + 2, False)

        build(n + 2, 0)
        correlate(n + 1, 1)
        return 0

    lax.fori_loop(0, total_units // 2 - 1, step, 0)
    build(total_units - 1, 1)
    correlate(total_units - 2, 0)
    correlate(total_units - 1, 1)

    energy = jnp.broadcast_to(jnp.sum(pw[...], axis=0, keepdims=True), (8, WIN + 128))
    for k in (1, 2, 4, 8, 16, 32, 64):
        energy = energy + pltpu.roll(energy, k, 1)
    by_time = 1.0 / jnp.sqrt(energy[0:1, 128:] * (1.0 / (CH * TLEN)) + EPSILON)
    mean = jnp.sum(tsq[...], axis=1, keepdims=True) * (1.0 / (CH * TLEN))
    by_tmpl = 1.0 / (CH * TLEN * jnp.sqrt(mean + EPSILON))
    back = 127 - iota((KEPT, 128), 1)
    for b in range(8):
        part = acc[:, 128 * b : 128 * b + 128] * by_tmpl * by_time[:, 128 * b : 128 * b + 128]
        out_ref[:, 128 * (7 - b) : 128 * (8 - b)] = lane_take(part, back)

    all_blocks().wait_send()
    for i in range(1, NY):
        main_copy(my, lax.rem(my + i, NY), i).wait_send()

    @pl.when(me > 0)
    def _():
        for i in range(NY):
            halo_copy(my, me - 1, lax.rem(my + i, NY), i).wait_send()


def shards(records, band_filter, templates, destinations, offsets, live_counts):
    vmem = pl.BlockSpec(memory_space=pltpu.VMEM)
    hbm = pl.BlockSpec(memory_space=pl.ANY)
    return pl.pallas_call(
        kernel,
        out_shape=jax.ShapeDtypeStruct((KEPT, WIN), F32),
        in_specs=[vmem, vmem, pl.BlockSpec(memory_space=pltpu.SMEM), vmem, hbm, hbm],
        out_specs=vmem,
        scratch_shapes=[
            pltpu.VMEM((EPAD, RECLEN), F32),
            pltpu.VMEM((KEPT, CH, TLEN), BF16),
            pltpu.VMEM((8, 128), F32),
            pltpu.VMEM((8, EPAD), jnp.int32),
            pltpu.VMEM((NTM * CAP + CAP, 128), F32),
            pltpu.VMEM((NTM, CAP, 128), BF16),
            pltpu.VMEM((NTM, CAP, 128), BF16),
            pltpu.VMEM((CH, KEPT, TLEN), BF16),
            pltpu.VMEM((KEPT, 128), F32),
            pltpu.VMEM((NY, UNITS, 16, WIN + 128), BF16),
            pltpu.VMEM((2, 16, WIN + 128), F32),
            pltpu.VMEM((16, WIN + 128), F32),
            pltpu.VMEM((2, UCH * TLEN, WIN), BF16),
            pltpu.VMEM((KEPT, WIN), F32),
            pltpu.SemaphoreType.DMA,
            pltpu.SemaphoreType.DMA((16,)),
            pltpu.SemaphoreType.DMA,
            pltpu.SemaphoreType.DMA,
            pltpu.SemaphoreType.DMA((2 * NY,)),
            pltpu.SemaphoreType.DMA((NY,)),
            pltpu.SemaphoreType.DMA((NY,)),
        ],
        compiler_params=pltpu.CompilerParams(
            collective_id=0, has_side_effects=True, vmem_limit_bytes=56 * 1024 * 1024
        ),
    )(destinations, offsets, live_counts, band_filter.reshape(1, TAPS), records, templates)


def solution(mesh):
    in_specs = (
        P("tmpl", "tm", None),
        P(),
        P("tmpl", None, None),
        P("tmpl", "tm"),
        P("tmpl", "tm"),
        P("tmpl", "tm"),
    )
    return jax.shard_map(
        shards, mesh=mesh, in_specs=in_specs, out_specs=P("tmpl", "tm"), check_vma=False
    )
```

time: 250 us -> 41.4 us (0.17)
  local copies, waits for them, and re-layouts: 147 us -> 2.31 us
  matrix products: 47.2 us -> 0 us
  Pallas kernels: 0 us -> 38.3 us
  blocking collectives: 23.7 us -> 0 us
  other arithmetic: 15.5 us -> 0 us
  starting transfers between devices: 8.53 us -> 0 us
  waiting for transfers between devices: 5.42 us -> 0 us
    while x120 -> x0, local copies, waits for them, and re-layouts: 104 us -> none
    dot_general x17 -> x0, matrix products: 47.2 us -> none  [the longest x8 33.4 us: add_group(): jnp.dot(block_tmpl, shifted, preferred_element_type=jnp.float32)]
    pallas_call x0 -> x1, Pallas kernels: none -> 38.3 us  [shards(): pl.pallas_call(kernel, out_shape=jax.ShapeDtypeStruct((KEPT, WIN), F32),...]
    all_to_all x1 -> x0, blocking collectives: 23.7 us -> none  [side_by_side(): lax.all_to_all(both, axis, split_axis=split_dim, concat_axis=concat_dim,...]
    unnamed x10 -> x1, local copies, waits for them, and re-layouts: 16.3 us -> 2.31 us
    scatter x2 -> x0, local copies, waits for them, and re-layouts: 8.31 us -> none  [the longest x1 4.21 us: arrange(): return empty.at[target].set(flat)[:-1]]
    another operation x14 -> x0, local copies, waits for them, and re-layouts: 7.62 us -> none  [the longest x8 6.82 us: add_group(): jnp.stack([lax.dynamic_slice_in_dim(piece, first + shift_at, window_len,...]
    scatter-add x1 -> x0, local copies, waits for them, and re-layouts: 6.88 us -> none  [shards(): tail_part = tail_part.at[:, :, rec_len // DEC - heads_len:].add(later)]
  transfers between devices with their start and end apart: 3 -> 0, of which waited for: 2 -> 0; matrix products, arithmetic and copies ran while one was open for 8% -> 0% of each run, Pallas kernels for 0% -> 0%
where the time goes in v1:
time: 41.4 us; the launch traced here: 41.2 us
  Pallas kernels  38.3 us (93%)
  local copies, waits for them, and re-layouts  2.31 us (6%)
  between operations  0.66 us (2%)
    pallas_call x1, Pallas kernels, shards(): pl.pallas_call(kernel, out_shape=jax.ShapeDtypeStruct((KEPT, WIN), F32),...  38.3 us
    unnamed x1, local copies, waits for them, and re-layouts  2.31 us

profile of v1, /device:TPU:1, one launch (start us, length us, event | category | flops | bytes accessed | tf_op | source)
XLA Modules:
  0.0 41.2 jit_solution(1975967575974121463)
XLA Ops:
  0.7 38.3 %shard_map.64 = f32[256,1024]{1,0:T(8,128)} custom-call(s32[1,576]{1,0:T(1,128)} %dest_ref.1, s32[1,576]{1,0:T(1,128)} %offs_ref.1, s32[1,1]{1,0:T(1,128)S(6)} %copy.8.live_ref, f32[1,65]{1,0:T(1,128)} %bitcast.1, f32[1,576,512]{2,1,0:T(8,128)} %rec_hbm.1, bf16[256,144,128]{2,1,0:T(8,128)(2,1)} %tmpl_hbm.1), custom_call_target="tpu_custom_call" | custom-call | tf_op jit(solution)/shard_map/pallas_call | solution.py:357
  38.9 2.3 %copy.9 = f32[256,1024]{1,0:T(8,128)} copy(f32[256,1024]{1,0:T(8,128)} %shard_map.64) | data formatting | bytes 2097152

commit v2 on v1

--- a/solution.py
+++ b/solution.py
@@ -17,6 +17,7 @@
 ENT = 576
 EPAD = 640
 CAP = 16
+WIRE = 10
 UNITS = 3
 UCH = 12
 KEPT = 256
@@ -24,6 +25,10 @@
 F32 = jnp.float32
 BF16 = jnp.bfloat16
 MESH = pl.DeviceIdType.MESH
+FAR_FIRST = sorted(
+    [(dx, dz, dc) for dx in range(4) for dz in range(8) for dc in range(2)][1:],
+    key=lambda d: -(min(d[0], 4 - d[0]) + min(d[1], 8 - d[1])),
+)
 NT = (((1,), (1,)), ((), ()))
 
 
@@ -36,13 +41,15 @@
 
 
 def kernel(
-    dest_ref,
-    offs_ref,
+    dest_hbm,
+    offs_hbm,
     live_ref,
-    band_ref,
+    band_hbm,
     rec_hbm,
     tmpl_hbm,
-    out_ref,
+    acc,
+    by_tmpl,
+    by_time,
     rec,
     tmpl,
     taps,
@@ -56,7 +63,9 @@
     g32,
     pw,
     hank,
-    acc,
+    dest_ref,
+    offs_ref,
+    band_ref,
     rec_sem,
     tmpl_sem,
     a_send,
@@ -68,8 +77,16 @@
     me = lax.axis_index("tm")
     my = lax.axis_index("tmpl")
 
-    rec_copy = pltpu.make_async_copy(rec_hbm.at[0], rec.at[pl.ds(0, ENT)], rec_sem)
+    rec_copy = pltpu.make_async_copy(rec_hbm.at[0], rec.at[pl.ds(0, ENT)], rec_sem.at[0])
+    small = [
+        pltpu.make_async_copy(dest_hbm, dest_ref, rec_sem.at[1]),
+        pltpu.make_async_copy(offs_hbm, offs_ref, rec_sem.at[2]),
+        pltpu.make_async_copy(band_hbm, band_ref, rec_sem.at[3]),
+    ]
+    for copy in small:
+        copy.start()
     rec_copy.start()
+    arr[...] = jnp.zeros(arr.shape, BF16)
     barrier = pltpu.get_barrier_semaphore()
 
     def greet(i, _):
@@ -98,6 +115,8 @@
 
     rec[ENT:EPAD, :] = jnp.zeros((EPAD - ENT, RECLEN), F32)
     rows[...] = jnp.full(rows.shape, -1, jnp.int32)
+    for copy in small:
+        copy.wait()
     rows[0:1, 0:ENT] = dest_ref[...]
     rows[1:2, 0:ENT] = offs_ref[...]
     entry = iota((1, EPAD), 1)
@@ -156,19 +175,18 @@
 
     def block_copy(to, frm):
         return pltpu.make_async_remote_copy(
-            src_ref=send.at[to],
-            dst_ref=arr.at[frm],
+            src_ref=send.at[to, pl.ds(0, WIRE)],
+            dst_ref=arr.at[frm, pl.ds(0, WIRE)],
             send_sem=a_send,
             recv_sem=a_recv,
             device_id={"tm": to},
             device_id_type=MESH,
         )
 
-    def send_block(i, _):
-        block_copy(lax.rem(me + i, NTM), me).start()
-        return 0
-
-    lax.fori_loop(1, NTM, send_block, 0)
+    x, z, core = me // 16, (me // 2) % 8, me % 2
+    for dx, dz, dc in FAR_FIRST:
+        to = ((x + dx) % 4) * 16 + ((z + dz) % 8) * 2 + (core + dc) % 2
+        block_copy(to, me).start()
     arr[me] = send[me]
 
     def order_templates(b, _):
@@ -184,11 +202,15 @@
         return 0
 
     lax.fori_loop(0, 16, order_templates, 0)
+    mean = jnp.sum(tsq[...], axis=1, keepdims=True) * (1.0 / (CH * TLEN))
+    by_tmpl[...] = jnp.broadcast_to(
+        1.0 / (CH * TLEN * jnp.sqrt(mean + EPSILON)), (KEPT, 128)
+    )
 
     def all_blocks():
         return pltpu.make_async_remote_copy(
-            src_ref=send.at[pl.ds(0, NTM - 1)],
-            dst_ref=arr.at[pl.ds(0, NTM - 1)],
+            src_ref=send.at[pl.ds(0, NTM - 1), pl.ds(0, WIRE)],
+            dst_ref=arr.at[pl.ds(0, NTM - 1), pl.ds(0, WIRE)],
             send_sem=a_send,
             recv_sem=a_recv,
             device_id={"tm": me},
@@ -327,19 +349,12 @@
 
     lax.fori_loop(0, total_units // 2 - 1, step, 0)
     build(total_units - 1, 1)
-    correlate(total_units - 2, 0)
-    correlate(total_units - 1, 1)
-
     energy = jnp.broadcast_to(jnp.sum(pw[...], axis=0, keepdims=True), (8, WIN + 128))
     for k in (1, 2, 4, 8, 16, 32, 64):
         energy = energy + pltpu.roll(energy, k, 1)
-    by_time = 1.0 / jnp.sqrt(energy[0:1, 128:] * (1.0 / (CH * TLEN)) + EPSILON)
-    mean = jnp.sum(tsq[...], axis=1, keepdims=True) * (1.0 / (CH * TLEN))
-    by_tmpl = 1.0 / (CH * TLEN * jnp.sqrt(mean + EPSILON))
-    back = 127 - iota((KEPT, 128), 1)
-    for b in range(8):
-        part = acc[:, 128 * b : 128 * b + 128] * by_tmpl * by_time[:, 128 * b : 128 * b + 128]
-        out_ref[:, 128 * (7 - b) : 128 * (8 - b)] = lane_take(part, back)
+    by_time[...] = 1.0 / jnp.sqrt(energy[:, 128:] * (1.0 / (CH * TLEN)) + EPSILON)
+    correlate(total_units - 2, 0)
+    correlate(total_units - 1, 1)
 
     all_blocks().wait_send()
     for i in range(1, NY):
@@ -351,14 +366,36 @@
             halo_copy(my, me - 1, lax.rem(my + i, NY), i).wait_send()
 
 
+def finish(acc, by_tmpl, by_time, out_hbm, stage, sem):
+    back = 127 - iota((KEPT, 128), 1)
+    copies = []
+    for b in range(8):
+        at = pl.ds(128 * (7 - b), 128)
+        part = acc[:, 128 * b : 128 * b + 128] * by_tmpl[...]
+        part = part * by_time[0:1, 128 * b : 128 * b + 128]
+        stage[b] = lane_take(part, back)
+        copies.append(pltpu.make_async_copy(stage.at[b], out_hbm.at[:, at], sem.at[b]))
+        copies[-1].start()
+    for copy in copies:
+        copy.wait()
+
+
+def in_hbm(x):
+    return pltpu.with_memory_space_constraint(x, pltpu.HBM)
+
+
 def shards(records, band_filter, templates, destinations, offsets, live_counts):
     vmem = pl.BlockSpec(memory_space=pltpu.VMEM)
-    hbm = pl.BlockSpec(memory_space=pl.ANY)
-    return pl.pallas_call(
+    hbm = pl.BlockSpec(memory_space=pltpu.HBM)
+    acc, by_tmpl, by_time = pl.pallas_call(
         kernel,
-        out_shape=jax.ShapeDtypeStruct((KEPT, WIN), F32),
-        in_specs=[vmem, vmem, pl.BlockSpec(memory_space=pltpu.SMEM), vmem, hbm, hbm],
-        out_specs=vmem,
+        out_shape=[
+            jax.ShapeDtypeStruct((KEPT, WIN), F32),
+            jax.ShapeDtypeStruct((KEPT, 128), F32),
+            jax.ShapeDtypeStruct((8, WIN), F32),
+        ],
+        in_specs=[hbm, hbm, pl.BlockSpec(memory_space=pltpu.SMEM), hbm, hbm, hbm],
+        out_specs=[vmem] * 3,
         scratch_shapes=[
             pltpu.VMEM((EPAD, RECLEN), F32),
             pltpu.VMEM((KEPT, CH, TLEN), BF16),
@@ -373,8 +410,10 @@
             pltpu.VMEM((2, 16, WIN + 128), F32),
             pltpu.VMEM((16, WIN + 128), F32),
             pltpu.VMEM((2, UCH * TLEN, WIN), BF16),
-            pltpu.VMEM((KEPT, WIN), F32),
-            pltpu.SemaphoreType.DMA,
+            pltpu.VMEM((1, ENT), jnp.int32),
+            pltpu.VMEM((1, ENT), jnp.int32),
+            pltpu.VMEM((1, TAPS), F32),
+            pltpu.SemaphoreType.DMA((4,)),
             pltpu.SemaphoreType.DMA((16,)),
             pltpu.SemaphoreType.DMA,
             pltpu.SemaphoreType.DMA,
@@ -383,9 +422,24 @@
             pltpu.SemaphoreType.DMA((NY,)),
         ],
         compiler_params=pltpu.CompilerParams(
-            collective_id=0, has_side_effects=True, vmem_limit_bytes=56 * 1024 * 1024
+            collective_id=0, has_side_effects=True, vmem_limit_bytes=52 * 1024 * 1024
         ),
-    )(destinations, offsets, live_counts, band_filter.reshape(1, TAPS), records, templates)
+    )(
+        in_hbm(destinations),
+        in_hbm(offsets),
+        live_counts,
+        in_hbm(band_filter.reshape(1, TAPS)),
+        in_hbm(records),
+        in_hbm(templates),
+    )
+    return pl.pallas_call(
+        finish,
+        out_shape=jax.ShapeDtypeStruct((KEPT, WIN), F32),
+        in_specs=[vmem] * 3,
+        out_specs=hbm,
+        scratch_shapes=[pltpu.VMEM((8, KEPT, 128), F32), pltpu.SemaphoreType.DMA((8,))],
+        compiler_params=pltpu.CompilerParams(vmem_limit_bytes=8 * 1024 * 1024),
+    )(acc, by_tmpl, by_time)
 
 
 def solution(mesh):

time: 41.4 us -> 37.3 us (0.901)
  local copies, waits for them, and re-layouts: 2.31 us -> 0 us
  Pallas kernels: 38.3 us -> 36.6 us
    unnamed x1 -> x0, local copies, waits for them, and re-layouts: 2.31 us -> none
    pallas_call x1 -> x2, Pallas kernels: 38.3 us -> 36.6 us  [the longest x1 35.5 us: shards(): pl.pallas_call(kernel, out_shape=[jax.ShapeDtypeStruct((KEPT, WIN), F32),...]
where the time goes in v2:
time: 37.3 us
  Pallas kernels  36.6 us (98%)
  between operations  0.66 us (2%)
    pallas_call x1, Pallas kernels, shards(): pl.pallas_call(kernel, out_shape=[jax.ShapeDtypeStruct((KEPT, WIN), F32),...  35.5 us
    pallas_call x1, Pallas kernels, shards(): pl.pallas_call(finish, out_shape=jax.ShapeDtypeStruct((KEPT, WIN), F32),...  1.13 us

profile of v2, /device:TPU:1, one launch (start us, length us, event | category | flops | bytes accessed | tf_op | source)
XLA Modules:
  0.0 37.3 jit_solution(2062469125878547453)
XLA Ops:
  0.7 35.5 %shard_map.64 = (f32[256,1024]{1,0:T(8,128)S(1)}, f32[256,128]{1,0:T(8,128)S(1)}, f32[8,1024]{1,0:T(8,128)S(1)}) custom-call(s32[1,576]{1,0:T(1,128)} %dest_hbm.1, s32[1,576]{1,0:T(1,128)} %offs_hbm.1, s32[1,1]{1,0:T(1,128)S(6)} %copy.7.live_ref, f32[1,65]{1,0:T(1,128)} %bitcast.1, f32[1,576,512]{2,1,0:T(8,128)} %rec_hbm.1, bf16[256,144,128]{2,1,0:T(8,128)(2,1)} %tmpl_hbm.1), custom_call_target="tpu_custom_call" | custom-call | tf_op jit(solution)/shard_map/pallas_call | solution.py:390
  36.1 1.1 %shard_map.65 = f32[256,1024]{1,0:T(8,128)} custom-call(f32[256,1024]{1,0:T(8,128)S(1)} %get-tuple-element.8.acc, f32[256,128]{1,0:T(8,128)S(1)} %get-tuple-element.9.by_tmpl, f32[8,1024]{1,0:T(8,128)S(1)} %get-tuple-element.10.by_time), custom_call_target="tpu_custom_call" | custom-call | tf_op jit(solution)/shard_map/pallas_call | solution.py:435

commit v3 on v2

--- a/solution.py
+++ b/solution.py
@@ -250,16 +250,16 @@
             + jnp.where(lane < 8, carry, 0.0)
         )
         carry = odd
-        gall[my, :, :, 128 * (b + 1) : 128 * (b + 2)] = block.astype(BF16).reshape(UNITS, 16, 128)
+        gall[my, :, b + 1] = block.astype(BF16).reshape(UNITS, 16, 128)
 
     @pl.when(me == NTM - 1)
     def _():
-        gall[:, :, :, 0:128] = jnp.zeros((NY, UNITS, 16, 128), BF16)
+        gall[:, :, 0] = jnp.zeros((NY, UNITS, 16, 128), BF16)
 
     def halo_copy(quarter, to_tm, to_y, k=0):
         return pltpu.make_async_remote_copy(
-            src_ref=gall.at[quarter, :, :, pl.ds(WIN, 128)],
-            dst_ref=gall.at[quarter, :, :, pl.ds(0, 128)],
+            src_ref=gall.at[quarter, :, 8, pl.ds(0, UCH)],
+            dst_ref=gall.at[quarter, :, 0, pl.ds(0, UCH)],
             send_sem=b_send.at[4 + k],
             recv_sem=halo_recv.at[quarter],
             device_id={"tm": to_tm, "tmpl": to_y},
@@ -268,8 +268,8 @@
 
     def main_copy(quarter, to_y, k=0):
         return pltpu.make_async_remote_copy(
-            src_ref=gall.at[quarter, :, :, pl.ds(128, WIN)],
-            dst_ref=gall.at[quarter, :, :, pl.ds(128, WIN)],
+            src_ref=gall.at[quarter, :, pl.ds(1, 8), pl.ds(0, UCH)],
+            dst_ref=gall.at[quarter, :, pl.ds(1, 8), pl.ds(0, UCH)],
             send_sem=b_send.at[k],
             recv_sem=main_recv.at[quarter],
             device_id={"tmpl": to_y},
@@ -281,7 +281,7 @@
         for i in (0, 1, 3, 2):
             halo_copy(my, me - 1, lax.rem(my + i, NY), i).start()
 
-    for i in (1, 3, 2):
+    for i in (1, 3):
         main_copy(my, lax.rem(my + i, NY), i).start()
 
     def quarter_of(n):
@@ -300,33 +300,56 @@
     hl = iota((16, 128), 1)
     hr = iota((16, 128), 0)
 
-    def build(n, side):
-        wide = gall[quarter_of(n), lax.rem(n, UNITS)].astype(F32)
-        g32[side] = wide
-        pw[...] += wide * wide
-        for i in range(UCH):
+    def widen(n, side, first, last):
+        for b in range(first, last):
+            at = slice(128 * b, 128 * b + 128)
+            wide = gall[quarter_of(n), lax.rem(n, UNITS), b].astype(F32)
+            wide = jnp.where(hr < UCH, wide, 0.0)
+            g32[side, :, at] = wide
+            pw[:, at] += wide * wide
+
+    def expand(side, channels, first, last):
+        for i in channels:
             line = [
                 jnp.broadcast_to(g32[side, i : i + 1, 128 * b : 128 * b + 128], (16, 128))
-                for b in range(9)
+                for b in range(first, last + 1)
             ]
             for s in range(8):
                 from_next = hl >= hr + 16 * s
                 turned = [pltpu.roll(x, 16 * s, 1, stride=1, stride_axis=0) for x in line]
-                for b in range(8):
+                for b in range(first, last):
                     at = i * 128 + 16 * s
                     hank[side, at : at + 16, 128 * b : 128 * b + 128] = jnp.where(
-                        from_next, turned[b + 1], turned[b]
+                        from_next, turned[b - first + 1], turned[b - first]
                     ).astype(BF16)
 
-    def correlate(n, side):
+    def build(n, side):
+        widen(n, side, 0, 9)
+        expand(side, range(UCH), 0, 8)
+
+    def correlate(n, side, lo=0, hi=WIN, channels=range(UCH)):
         c0 = quarter_of(n) * (CH // NY) + lax.rem(n, UNITS) * UCH
-        left = jnp.concatenate([wts[c0 + i] for i in range(UCH)], axis=1)
-        acc[...] += jnp.dot(left, hank[side], preferred_element_type=F32)
+        left = jnp.concatenate([wts[c0 + i] for i in channels], axis=1)
+        deep = slice(channels[0] * TLEN, (channels[-1] + 1) * TLEN)
+        acc[:, lo:hi] += jnp.dot(left, hank[side, deep, lo:hi], preferred_element_type=F32)
 
     acc[...] = jnp.zeros(acc.shape, F32)
     pw[...] = jnp.zeros(pw.shape, F32)
+    widen(0, 0, 1, 9)
+    thirds = [range(4 * i, 4 * i + 4) for i in range(3)]
+    expand(0, thirds[0], 1, 8)
+    for i in range(3):
+        if i < 2:
+            expand(0, thirds[i + 1], 1, 8)
+        correlate(0, 0, 256, WIN, thirds[i])
     arrive(0, True)
-    build(0, 0)
+    widen(0, 0, 0, 1)
+    expand(0, range(UCH), 0, 1)
+    build(1, 1)
+    correlate(0, 0, 0, 256)
+    main_copy(my, lax.rem(my + 2, NY), 2).start()
+    build(2, 0)
+    correlate(1, 1)
     total_units = NY * UNITS
 
     def step(it, _):
@@ -347,7 +370,7 @@
         correlate(n + 1, 1)
         return 0
 
-    lax.fori_loop(0, total_units // 2 - 1, step, 0)
+    lax.fori_loop(1, total_units // 2 - 1, step, 0)
     build(total_units - 1, 1)
     energy = jnp.broadcast_to(jnp.sum(pw[...], axis=0, keepdims=True), (8, WIN + 128))
     for k in (1, 2, 4, 8, 16, 32, 64):
@@ -406,7 +429,7 @@
             pltpu.VMEM((NTM, CAP, 128), BF16),
             pltpu.VMEM((CH, KEPT, TLEN), BF16),
             pltpu.VMEM((KEPT, 128), F32),
-            pltpu.VMEM((NY, UNITS, 16, WIN + 128), BF16),
+            pltpu.VMEM((NY, UNITS, 9, 16, 128), BF16),
             pltpu.VMEM((2, 16, WIN + 128), F32),
             pltpu.VMEM((16, WIN + 128), F32),
             pltpu.VMEM((2, UCH * TLEN, WIN), BF16),

time: 37.3 us -> 36.6 us (0.981)
  Pallas kernels: 36.6 us -> 35.8 us
    pallas_call x1, Pallas kernels: 35.5 us -> 34.7 us  [shards(): pl.pallas_call(kernel, out_shape=[jax.ShapeDtypeStruct((KEPT, WIN), F32),...]
where the time goes in v3:
time: 36.6 us; the launch traced here: 36.5 us
  Pallas kernels  35.8 us (98%)
  between operations  0.66 us (2%)
    pallas_call x1, Pallas kernels, shards(): pl.pallas_call(kernel, out_shape=[jax.ShapeDtypeStruct((KEPT, WIN), F32),...  34.7 us
    pallas_call x1, Pallas kernels, shards(): pl.pallas_call(finish, out_shape=jax.ShapeDtypeStruct((KEPT, WIN), F32),...  1.13 us

profile of v3, /device:TPU:1, one launch (start us, length us, event | category | flops | bytes accessed | tf_op | source)
XLA Modules:
  0.0 36.5 jit_solution(14540242317505821042)
XLA Ops:
  0.7 34.7 %shard_map.64 = (f32[256,1024]{1,0:T(8,128)S(1)}, f32[256,128]{1,0:T(8,128)S(1)}, f32[8,1024]{1,0:T(8,128)S(1)}) custom-call(s32[1,576]{1,0:T(1,128)} %dest_hbm.1, s32[1,576]{1,0:T(1,128)} %offs_hbm.1, s32[1,1]{1,0:T(1,128)S(6)} %copy.7.live_ref, f32[1,65]{1,0:T(1,128)} %bitcast.1, f32[1,576,512]{2,1,0:T(8,128)} %rec_hbm.1, bf16[256,144,128]{2,1,0:T(8,128)(2,1)} %tmpl_hbm.1), custom_call_target="tpu_custom_call" | custom-call | tf_op jit(solution)/shard_map/pallas_call | solution.py:413
  35.3 1.1 %shard_map.65 = f32[256,1024]{1,0:T(8,128)} custom-call(f32[256,1024]{1,0:T(8,128)S(1)} %get-tuple-element.8.acc, f32[256,128]{1,0:T(8,128)S(1)} %get-tuple-element.9.by_tmpl, f32[8,1024]{1,0:T(8,128)S(1)} %get-tuple-element.10.by_time), custom_call_target="tpu_custom_call" | custom-call | tf_op jit(solution)/shard_map/pallas_call | solution.py:458

commit v4 on v3

--- a/solution.py
+++ b/solution.py
@@ -50,6 +50,8 @@
     acc,
     by_tmpl,
     by_time,
+    hank1,
+    last_wts,
     rec,
     tmpl,
     taps,
@@ -62,7 +64,7 @@
     gall,
     g32,
     pw,
-    hank,
+    hank0,
     dest_ref,
     offs_ref,
     band_ref,
@@ -89,13 +91,12 @@
     arr[...] = jnp.zeros(arr.shape, BF16)
     barrier = pltpu.get_barrier_semaphore()
 
-    def greet(i, _):
-        pl.semaphore_signal(
-            barrier, inc=1, device_id={"tm": lax.rem(me + i, NTM)}, device_id_type=MESH
-        )
-        return 0
-
-    lax.fori_loop(1, NTM, greet, 0)
+    x, z, core = me // 16, (me // 2) % 8, me % 2
+    partners = [
+        ((x + dx) % 4) * 16 + ((z + dz) % 8) * 2 + (core + dc) % 2 for dx, dz, dc in FAR_FIRST
+    ]
+    for to in partners:
+        pl.semaphore_signal(barrier, inc=1, device_id={"tm": to}, device_id_type=MESH)
     for i in range(1, NY):
         other = lax.rem(my + i, NY)
         pl.semaphore_signal(barrier, inc=1, device_id={"tmpl": other}, device_id_type=MESH)
@@ -148,9 +149,10 @@
     data = rec[...]
     data_hi = data.astype(BF16)
     data_lo = (data - data_hi.astype(F32)).astype(BF16)
-    parts = lax.dot_general(band_hi, data_hi, NT, preferred_element_type=F32)
-    parts += lax.dot_general(band_hi, data_lo, NT, preferred_element_type=F32)
-    parts += lax.dot_general(band_lo, data_hi, NT, preferred_element_type=F32)
+    both = jnp.concatenate([band_hi, band_lo], axis=0)
+    both = lax.dot_general(both, data_hi, NT, preferred_element_type=F32)
+    parts = lax.dot_general(band_hi, data_lo, NT, preferred_element_type=F32)
+    parts += both[0:80] + both[80:160]
     row = iota((80, EPAD), 0)
     parts = jnp.where(row == 72, jnp.broadcast_to(chan.astype(F32), (80, EPAD)), parts)
     parts = jnp.where(row == 73, jnp.broadcast_to(slot.astype(F32), (80, EPAD)), parts)
@@ -183,9 +185,7 @@
             device_id_type=MESH,
         )
 
-    x, z, core = me // 16, (me // 2) % 8, me % 2
-    for dx, dz, dc in FAR_FIRST:
-        to = ((x + dx) % 4) * 16 + ((z + dz) % 8) * 2 + (core + dc) % 2
+    for to in partners:
         block_copy(to, me).start()
     arr[me] = send[me]
 
@@ -297,6 +297,8 @@
         def _():
             halo_copy(quarter, me, my).wait_recv()
 
+    hank = (hank0, hank1)
+    last = NY * UNITS - 1
     hl = iota((16, 128), 1)
     hr = iota((16, 128), 0)
 
@@ -319,7 +321,7 @@
                 turned = [pltpu.roll(x, 16 * s, 1, stride=1, stride_axis=0) for x in line]
                 for b in range(first, last):
                     at = i * 128 + 16 * s
-                    hank[side, at : at + 16, 128 * b : 128 * b + 128] = jnp.where(
+                    hank[side][at : at + 16, 128 * b : 128 * b + 128] = jnp.where(
                         from_next, turned[b - first + 1], turned[b - first]
                     ).astype(BF16)
 
@@ -330,8 +332,13 @@
     def correlate(n, side, lo=0, hi=WIN, channels=range(UCH)):
         c0 = quarter_of(n) * (CH // NY) + lax.rem(n, UNITS) * UCH
         left = jnp.concatenate([wts[c0 + i] for i in channels], axis=1)
+        if n is last:
+            last_wts[...] = left
+            return
         deep = slice(channels[0] * TLEN, (channels[-1] + 1) * TLEN)
-        acc[:, lo:hi] += jnp.dot(left, hank[side, deep, lo:hi], preferred_element_type=F32)
+        acc[:, lo:hi] += jnp.dot(
+            left, hank[side][deep, lo:hi], preferred_element_type=F32
+        )
 
     acc[...] = jnp.zeros(acc.shape, F32)
     pw[...] = jnp.zeros(pw.shape, F32)
@@ -350,7 +357,6 @@
     main_copy(my, lax.rem(my + 2, NY), 2).start()
     build(2, 0)
     correlate(1, 1)
-    total_units = NY * UNITS
 
     def step(it, _):
         n = 2 * it
@@ -370,14 +376,14 @@
         correlate(n + 1, 1)
         return 0
 
-    lax.fori_loop(1, total_units // 2 - 1, step, 0)
-    build(total_units - 1, 1)
+    lax.fori_loop(1, NY * UNITS // 2 - 1, step, 0)
+    build(last, 1)
     energy = jnp.broadcast_to(jnp.sum(pw[...], axis=0, keepdims=True), (8, WIN + 128))
     for k in (1, 2, 4, 8, 16, 32, 64):
         energy = energy + pltpu.roll(energy, k, 1)
     by_time[...] = 1.0 / jnp.sqrt(energy[:, 128:] * (1.0 / (CH * TLEN)) + EPSILON)
-    correlate(total_units - 2, 0)
-    correlate(total_units - 1, 1)
+    correlate(last - 1, 0)
+    correlate(last, 1)
 
     all_blocks().wait_send()
     for i in range(1, NY):
@@ -389,16 +395,20 @@
             halo_copy(my, me - 1, lax.rem(my + i, NY), i).wait_send()
 
 
-def finish(acc, by_tmpl, by_time, out_hbm, stage, sem):
+def finish(acc, by_tmpl, by_time, hank, wts, out_hbm, stage, sem):
     back = 127 - iota((KEPT, 128), 1)
     copies = []
-    for b in range(8):
-        at = pl.ds(128 * (7 - b), 128)
-        part = acc[:, 128 * b : 128 * b + 128] * by_tmpl[...]
-        part = part * by_time[0:1, 128 * b : 128 * b + 128]
-        stage[b] = lane_take(part, back)
-        copies.append(pltpu.make_async_copy(stage.at[b], out_hbm.at[:, at], sem.at[b]))
-        copies[-1].start()
+    for two in range(4):
+        span = slice(256 * two, 256 * two + 256)
+        corr = acc[:, span] + jnp.dot(wts[...], hank[:, span], preferred_element_type=F32)
+        for half in range(2):
+            b = 2 * two + half
+            part = corr[:, 128 * half : 128 * half + 128] * by_tmpl[...]
+            part = part * by_time[0:1, 128 * b : 128 * b + 128]
+            stage[b] = lane_take(part, back)
+            at = pl.ds(128 * (7 - b), 128)
+            copies.append(pltpu.make_async_copy(stage.at[b], out_hbm.at[:, at], sem.at[b]))
+            copies[-1].start()
     for copy in copies:
         copy.wait()
 
@@ -410,15 +420,17 @@
 def shards(records, band_filter, templates, destinations, offsets, live_counts):
     vmem = pl.BlockSpec(memory_space=pltpu.VMEM)
     hbm = pl.BlockSpec(memory_space=pltpu.HBM)
-    acc, by_tmpl, by_time = pl.pallas_call(
+    results = pl.pallas_call(
         kernel,
         out_shape=[
             jax.ShapeDtypeStruct((KEPT, WIN), F32),
             jax.ShapeDtypeStruct((KEPT, 128), F32),
             jax.ShapeDtypeStruct((8, WIN), F32),
+            jax.ShapeDtypeStruct((UCH * TLEN, WIN), BF16),
+            jax.ShapeDtypeStruct((KEPT, UCH * TLEN), BF16),
         ],
         in_specs=[hbm, hbm, pl.BlockSpec(memory_space=pltpu.SMEM), hbm, hbm, hbm],
-        out_specs=[vmem] * 3,
+        out_specs=[vmem] * 5,
         scratch_shapes=[
             pltpu.VMEM((EPAD, RECLEN), F32),
             pltpu.VMEM((KEPT, CH, TLEN), BF16),
@@ -432,7 +444,7 @@
             pltpu.VMEM((NY, UNITS, 9, 16, 128), BF16),
             pltpu.VMEM((2, 16, WIN + 128), F32),
             pltpu.VMEM((16, WIN + 128), F32),
-            pltpu.VMEM((2, UCH * TLEN, WIN), BF16),
+            pltpu.VMEM((UCH * TLEN, WIN), BF16),
             pltpu.VMEM((1, ENT), jnp.int32),
             pltpu.VMEM((1, ENT), jnp.int32),
             pltpu.VMEM((1, TAPS), F32),
@@ -445,7 +457,7 @@
             pltpu.SemaphoreType.DMA((NY,)),
         ],
         compiler_params=pltpu.CompilerParams(
-            collective_id=0, has_side_effects=True, vmem_limit_bytes=52 * 1024 * 1024
+            collective_id=0, has_side_effects=True, vmem_limit_bytes=40 * 1024 * 1024
         ),
     )(
         in_hbm(destinations),
@@ -458,11 +470,11 @@
     return pl.pallas_call(
         finish,
         out_shape=jax.ShapeDtypeStruct((KEPT, WIN), F32),
-        in_specs=[vmem] * 3,
+        in_specs=[vmem] * 5,
         out_specs=hbm,
         scratch_shapes=[pltpu.VMEM((8, KEPT, 128), F32), pltpu.SemaphoreType.DMA((8,))],
         compiler_params=pltpu.CompilerParams(vmem_limit_bytes=8 * 1024 * 1024),
-    )(acc, by_tmpl, by_time)
+    )(*results)
 
 
 def solution(mesh):

time: 36.6 us -> 36.8 us (level)
    pallas_call x1, Pallas kernels: 1.13 us -> 2 us  [shards(): pl.pallas_call(finish, out_shape=jax.ShapeDtypeStruct((KEPT, WIN), F32),...]
    pallas_call x1, Pallas kernels: 34.7 us -> 34 us  [shards(): pl.pallas_call(kernel, out_shape=[jax.ShapeDtypeStruct((KEPT, WIN), F32),...]
where the time goes in v4:
time: 36.8 us; the launch traced here: 36.7 us
  Pallas kernels  36 us (98%)
  between operations  0.66 us (2%)
    pallas_call x1, Pallas kernels, shards(): pl.pallas_call(kernel, out_shape=[jax.ShapeDtypeStruct((KEPT, WIN), F32),...  34 us
    pallas_call x1, Pallas kernels, shards(): pl.pallas_call(finish, out_shape=jax.ShapeDtypeStruct((KEPT, WIN), F32),...  2 us

profile of v4, /device:TPU:1, one launch (start us, length us, event | category | flops | bytes accessed | tf_op | source)
XLA Modules:
  0.0 36.7 jit_solution(379273641917615188)
XLA Ops:
  0.7 34.0 %shard_map.64 = (f32[256,1024]{1,0:T(8,128)S(1)}, f32[256,128]{1,0:T(8,128)S(1)}, f32[8,1024]{1,0:T(8,128)S(1)}, bf16[1536,1024]{1,0:T(8,128)(2,1)S(1)}, bf16[256,1536]{1,0:T(8,128)(2,1)S(1)}) custom-call(s32[1,576]{1,0:T(1,128)} %dest_hbm.1, s32[1,576]{1,0:T(1,128)} %offs_hbm.1, s32[1,1]{1,0:T(1,128)S(6)} %copy.7.live_ref, f32[1,65]{1,0:T(1,128)} %bitcast.1, ...), custom_call_target="tpu_custom_call" | custom-call | tf_op jit(solution)/shard_map/pallas_call | solution.py:423
  34.7 2.0 %shard_map.65 = f32[256,1024]{1,0:T(8,128)} custom-call(f32[256,1024]{1,0:T(8,128)S(1)} %get-tuple-element.10.acc, f32[256,128]{1,0:T(8,128)S(1)} %get-tuple-element.11.by_tmpl, f32[8,1024]{1,0:T(8,128)S(1)} %get-tuple-element.12.by_time, bf16[1536,1024]{1,0:T(8,128)(2,1)S(1)} %get-tuple-element.13.hank, bf16[256,1536]{1,0:T(8,128)(2,1)S(1)} %get-tuple-element.14.wts), custom_call_target="tpu_custom_call" | custom-call | tf_op jit(solution)/shard_map/pallas_call | solution.py:470

commit v5 on v3

--- a/solution.py
+++ b/solution.py
@@ -89,13 +89,12 @@
     arr[...] = jnp.zeros(arr.shape, BF16)
     barrier = pltpu.get_barrier_semaphore()
 
-    def greet(i, _):
-        pl.semaphore_signal(
-            barrier, inc=1, device_id={"tm": lax.rem(me + i, NTM)}, device_id_type=MESH
-        )
-        return 0
-
-    lax.fori_loop(1, NTM, greet, 0)
+    x, z, core = me // 16, (me // 2) % 8, me % 2
+    partners = [
+        ((x + dx) % 4) * 16 + ((z + dz) % 8) * 2 + (core + dc) % 2 for dx, dz, dc in FAR_FIRST
+    ]
+    for to in partners:
+        pl.semaphore_signal(barrier, inc=1, device_id={"tm": to}, device_id_type=MESH)
     for i in range(1, NY):
         other = lax.rem(my + i, NY)
         pl.semaphore_signal(barrier, inc=1, device_id={"tmpl": other}, device_id_type=MESH)
@@ -148,9 +147,10 @@
     data = rec[...]
     data_hi = data.astype(BF16)
     data_lo = (data - data_hi.astype(F32)).astype(BF16)
-    parts = lax.dot_general(band_hi, data_hi, NT, preferred_element_type=F32)
-    parts += lax.dot_general(band_hi, data_lo, NT, preferred_element_type=F32)
-    parts += lax.dot_general(band_lo, data_hi, NT, preferred_element_type=F32)
+    both = jnp.concatenate([band_hi, band_lo], axis=0)
+    both = lax.dot_general(both, data_hi, NT, preferred_element_type=F32)
+    parts = lax.dot_general(band_hi, data_lo, NT, preferred_element_type=F32)
+    parts += both[0:80] + both[80:160]
     row = iota((80, EPAD), 0)
     parts = jnp.where(row == 72, jnp.broadcast_to(chan.astype(F32), (80, EPAD)), parts)
     parts = jnp.where(row == 73, jnp.broadcast_to(slot.astype(F32), (80, EPAD)), parts)
@@ -183,9 +183,7 @@
             device_id_type=MESH,
         )
 
-    x, z, core = me // 16, (me // 2) % 8, me % 2
-    for dx, dz, dc in FAR_FIRST:
-        to = ((x + dx) % 4) * 16 + ((z + dz) % 8) * 2 + (core + dc) % 2
+    for to in partners:
         block_copy(to, me).start()
     arr[me] = send[me]
 
@@ -278,11 +276,15 @@
 
     @pl.when(me > 0)
     def _():
-        for i in (0, 1, 3, 2):
-            halo_copy(my, me - 1, lax.rem(my + i, NY), i).start()
+        halo_copy(my, me - 1, my, 0).start()
 
     for i in (1, 3):
         main_copy(my, lax.rem(my + i, NY), i).start()
+
+    @pl.when(me > 0)
+    def _():
+        for i in (1, 3, 2):
+            halo_copy(my, me - 1, lax.rem(my + i, NY), i).start()
 
     def quarter_of(n):
         step = n // UNITS
@@ -315,12 +317,12 @@
                 for b in range(first, last + 1)
             ]
             for s in range(8):
-                from_next = hl >= hr + 16 * s
-                turned = [pltpu.roll(x, 16 * s, 1, stride=1, stride_axis=0) for x in line]
+                from_last = hl + hr >= 128 - 16 * s
                 for b in range(first, last):
+                    mixed = jnp.where(from_last, line[b - first], line[b - first + 1])
                     at = i * 128 + 16 * s
-                    hank[side, at : at + 16, 128 * b : 128 * b + 128] = jnp.where(
-                        from_next, turned[b - first + 1], turned[b - first]
+                    hank[side, at : at + 16, 128 * b : 128 * b + 128] = pltpu.roll(
+                        mixed, 16 * s, 1, stride=1, stride_axis=0
                     ).astype(BF16)
 
     def build(n, side):

time: 36.6 us -> 36.7 us (level)
  no operation moved by 1% of the time
where the time goes in v5:
time: 36.7 us; the launch traced here: 36.6 us
  Pallas kernels  36 us (98%)
  between operations  0.66 us (2%)
    pallas_call x1, Pallas kernels, shards(): pl.pallas_call(kernel, out_shape=[jax.ShapeDtypeStruct((KEPT, WIN), F32),...  34.8 us
    pallas_call x1, Pallas kernels, shards(): pl.pallas_call(finish, out_shape=jax.ShapeDtypeStruct((KEPT, WIN), F32),...  1.13 us

profile of v5, /device:TPU:1, one launch (start us, length us, event | category | flops | bytes accessed | tf_op | source)
XLA Modules:
  0.0 36.6 jit_solution(14977841641476207973)
XLA Ops:
  0.7 34.8 %shard_map.64 = (f32[256,1024]{1,0:T(8,128)S(1)}, f32[256,128]{1,0:T(8,128)S(1)}, f32[8,1024]{1,0:T(8,128)S(1)}) custom-call(s32[1,576]{1,0:T(1,128)} %dest_hbm.1, s32[1,576]{1,0:T(1,128)} %offs_hbm.1, s32[1,1]{1,0:T(1,128)S(6)} %copy.7.live_ref, f32[1,65]{1,0:T(1,128)} %bitcast.1, f32[1,576,512]{2,1,0:T(8,128)} %rec_hbm.1, bf16[256,144,128]{2,1,0:T(8,128)(2,1)} %tmpl_hbm.1), custom_call_target="tpu_custom_call" | custom-call | tf_op jit(solution)/shard_map/pallas_call | solution.py:415
  35.5 1.1 %shard_map.65 = f32[256,1024]{1,0:T(8,128)} custom-call(f32[256,1024]{1,0:T(8,128)S(1)} %get-tuple-element.8.acc, f32[256,128]{1,0:T(8,128)S(1)} %get-tuple-element.9.by_tmpl, f32[8,1024]{1,0:T(8,128)S(1)} %get-tuple-element.10.by_time), custom_call_target="tpu_custom_call" | custom-call | tf_op jit(solution)/shard_map/pallas_call | solution.py:460

commit v6 on v5

--- a/solution.py
+++ b/solution.py
@@ -77,7 +77,12 @@
     me = lax.axis_index("tm")
     my = lax.axis_index("tmpl")
 
-    rec_copy = pltpu.make_async_copy(rec_hbm.at[0], rec.at[pl.ds(0, ENT)], rec_sem.at[0])
+    pieces = [
+        pltpu.make_async_copy(
+            rec_hbm.at[0, pl.ds(144 * i, 144)], rec.at[pl.ds(144 * i, 144)], rec_sem.at[4 + i]
+        )
+        for i in range(4)
+    ]
     small = [
         pltpu.make_async_copy(dest_hbm, dest_ref, rec_sem.at[1]),
         pltpu.make_async_copy(offs_hbm, offs_ref, rec_sem.at[2]),
@@ -85,7 +90,8 @@
     ]
     for copy in small:
         copy.start()
-    rec_copy.start()
+    for copy in pieces:
+        copy.start()
     arr[...] = jnp.zeros(arr.shape, BF16)
     barrier = pltpu.get_barrier_semaphore()
 
@@ -108,9 +114,6 @@
     def tmpl_copy(b):
         part = pl.ds(pl.multiple_of(b * 16, 16), 16)
         return pltpu.make_async_copy(tmpl_hbm.at[part], tmpl.at[part], tmpl_sem.at[b])
-
-    for b in range(16):
-        tmpl_copy(b).start()
 
     rec[ENT:EPAD, :] = jnp.zeros((EPAD - ENT, RECLEN), F32)
     rows[...] = jnp.full(rows.shape, -1, jnp.int32)
@@ -143,7 +146,10 @@
     band_hi = band.astype(BF16)
     band_lo = (band - band_hi.astype(F32)).astype(BF16)
 
-    rec_copy.wait()
+    for copy in pieces:
+        copy.wait()
+    for b in range(16):
+        tmpl_copy(b).start()
     data = rec[...]
     data_hi = data.astype(BF16)
     data_lo = (data - data_hi.astype(F32)).astype(BF16)
@@ -438,7 +444,7 @@
             pltpu.VMEM((1, ENT), jnp.int32),
             pltpu.VMEM((1, ENT), jnp.int32),
             pltpu.VMEM((1, TAPS), F32),
-            pltpu.SemaphoreType.DMA((4,)),
+            pltpu.SemaphoreType.DMA((8,)),
             pltpu.SemaphoreType.DMA((16,)),
             pltpu.SemaphoreType.DMA,
             pltpu.SemaphoreType.DMA,

time: 36.7 us -> 36.7 us (level)
  no operation moved by 1% of the time
where the time goes in v6:
time: 36.7 us; the launch traced here: 36.6 us
  Pallas kernels  36 us (98%)
  between operations  0.66 us (2%)
    pallas_call x1, Pallas kernels, shards(): pl.pallas_call(kernel, out_shape=[jax.ShapeDtypeStruct((KEPT, WIN), F32),...  34.8 us
    pallas_call x1, Pallas kernels, shards(): pl.pallas_call(finish, out_shape=jax.ShapeDtypeStruct((KEPT, WIN), F32),...  1.13 us

profile of v6, /device:TPU:1, one launch (start us, length us, event | category | flops | bytes accessed | tf_op | source)
XLA Modules:
  0.0 36.6 jit_solution(4664381464210989083)
XLA Ops:
  0.7 34.8 %shard_map.64 = (f32[256,1024]{1,0:T(8,128)S(1)}, f32[256,128]{1,0:T(8,128)S(1)}, f32[8,1024]{1,0:T(8,128)S(1)}) custom-call(s32[1,576]{1,0:T(1,128)} %dest_hbm.1, s32[1,576]{1,0:T(1,128)} %offs_hbm.1, s32[1,1]{1,0:T(1,128)S(6)} %copy.7.live_ref, f32[1,65]{1,0:T(1,128)} %bitcast.1, f32[1,576,512]{2,1,0:T(8,128)} %rec_hbm.1, bf16[256,144,128]{2,1,0:T(8,128)(2,1)} %tmpl_hbm.1), custom_call_target="tpu_custom_call" | custom-call | tf_op jit(solution)/shard_map/pallas_call | solution.py:421
  35.5 1.1 %shard_map.65 = f32[256,1024]{1,0:T(8,128)} custom-call(f32[256,1024]{1,0:T(8,128)S(1)} %get-tuple-element.8.acc, f32[256,128]{1,0:T(8,128)S(1)} %get-tuple-element.9.by_tmpl, f32[8,1024]{1,0:T(8,128)S(1)} %get-tuple-element.10.by_time), custom_call_target="tpu_custom_call" | custom-call | tf_op jit(solution)/shard_map/pallas_call | solution.py:466
